TPU v7x, 256 devices: a whole 4x4x8 slice. The times are simulated.
256 devices in a mesh: vel: 32 (over x, z), gx: 8 (over y, core).
Axes of the slice: x: 4, y: 4, z: 8, core: 2. Of those that a mesh axis runs over, the one named last changes fastest.
Arguments:
- distribution: float32 [13824, 128, 128], P('vel', 'gx')
- speeds: float32 [3, 13824], P(None, 'vel'), may hold values from 0.03 to 3, as said below
- weights: float32 [13824], P('vel'), may hold values from 3.616898e-05 to 0.00014467593
- octant: int32 [32], P('vel'), may hold values from 0 to 3, as said below
- inverses: float32 [12, 128, 128], replicated, as said below
- inflow: float32 [13824, 128], P('vel'), may hold values from -6 to 6
- solid_cells: int32 [128, 128], P('gx'), may hold values 0 or 1
Outputs:
- new_distribution: float32 [13824, 128, 128], P('vel', 'gx')
- moment_fields: float32 [8, 128, 128], P(None, 'gx')
Inputs may be any that keep to these rules, and one draw needn't show every extreme that they name: `octant`: every value occurs among the shards. `speeds`: all magnitudes are positive. `inverses`: each inverse is lower triangular.
All inputs are finite; a program needn't handle non-finite values. No bound on the sum of `solid_cells` on one device may be relied on, other than what follows from the above.
Results may differ from a plain program's by a relative error of at most 0.0003.
Values sent between devices are 32-bit elements; how exact they have to be, the bound alone decides.
A program may use at most 64 MiB of HBM per device.

v0:
```python
import jax
import jax.numpy as jnp
from jax import lax
from jax.sharding import PartitionSpec as P

SWEEPS = 2


PRECISE = lax.Precision.HIGHEST
SHAKHOV = 4.0 / 45.0
KNUDSEN_STEP = 0.004
ABSORB = 0.3


def from_behind(block, axis, distance):
    devices = range(lax.axis_size(axis))
    route = [(i - distance, i) for i in devices if i - distance in devices]
    return lax.ppermute(block, axis, route)


def signed_speeds(speed_block, quadrant):
    velocity_count = speed_block.shape[1]
    position = jnp.arange(velocity_count, dtype=jnp.int32)
    sign_x = jnp.where(position < velocity_count // 2, 1.0, -1.0).astype(jnp.float32)
    sign_y = (1 - 2 * (quadrant % 2)).astype(jnp.float32)
    sign_z = (1 - 2 * (quadrant // 2)).astype(jnp.float32)
    return (speed_block[0] * sign_x, speed_block[1] * sign_y, speed_block[2] * sign_z)


def bases(speed_x, speed_y, speed_z):
    energy = speed_x * speed_x + speed_y * speed_y + speed_z * speed_z
    flux_part = energy - 2.5
    unity = jnp.ones_like(speed_x)
    moment_rows = jnp.stack(
        [
            unity,
            speed_x,
            speed_y,
            speed_z,
            energy * (2.0 / 3.0) - 1.0,
            speed_x * flux_part,
            speed_y * flux_part,
            speed_z * flux_part,
        ]
    )
    source_rows = jnp.stack(
        [
            unity,
            2.0 * speed_x,
            2.0 * speed_y,
            2.0 * speed_z,
            energy - 1.5,
            SHAKHOV * speed_x * flux_part,
            SHAKHOV * speed_y * flux_part,
            SHAKHOV * speed_z * flux_part,
        ]
    )
    return (moment_rows, source_rows)


def summed_moments(field, weighted_rows):
    flattened = field.reshape(field.shape[0], field.shape[1] * field.shape[2])
    partial_sum = jnp.dot(
        weighted_rows, flattened, precision=PRECISE, preferred_element_type=jnp.float32
    )
    return lax.psum(partial_sum, "vel")


def local_march(relaxed, rates, retained, backward):
    columns_count = relaxed.shape[1]
    if backward:
        visit = list(range(columns_count - 1, -1, -1))
    else:
        visit = list(range(columns_count))
    running = jnp.zeros((relaxed.shape[0], relaxed.shape[2]), jnp.float32)
    stored = [None] * columns_count
    for column in visit:
        running = (
            rates * retained[column][None, :] * running + (1.0 - rates) * relaxed[:, column, :]
        )
        stored[column] = running
    return (jnp.stack(stored, axis=1), running)


def per_device(distribution, speeds, weights, octant, inverses, inflow, solid_cells):
    velocity_count, cells_x, cells_y = distribution.shape
    half_count = velocity_count // 2
    classes = inverses.shape[0]
    quadrant = octant[0]
    speed_x, speed_y, speed_z = signed_speeds(speeds, quadrant)
    moment_rows, source_rows = bases(speed_x, speed_y, speed_z)
    weighted_rows = moment_rows * weights[None, :]
    retained = 1.0 - ABSORB * solid_cells.astype(jnp.float32)
    operator = jnp.where(quadrant % 2 == 0, inverses, inverses[:, ::-1, ::-1])
    rate_vector = jnp.abs(speed_x) / (jnp.abs(speed_x) + KNUDSEN_STEP)
    forward_rates = rate_vector[:half_count, None]
    backward_rates = rate_vector[half_count:, None]
    sections = lax.axis_size("gx")
    section = lax.axis_index("gx")
    forward_steps = jnp.arange(1, cells_x + 1, dtype=jnp.int32).astype(jnp.float32)
    backward_steps = jnp.arange(cells_x, 0, -1, dtype=jnp.int32).astype(jnp.float32)
    forward_kept = jnp.cumprod(retained, axis=0)
    backward_kept = jnp.cumprod(retained[::-1], axis=0)[::-1]
    forward_reach = rate_vector[:half_count, None] ** forward_steps[None, :]
    backward_reach = rate_vector[half_count:, None] ** backward_steps[None, :]
    forward_span = forward_reach[:, cells_x - 1][:, None] * forward_kept[cells_x - 1][None, :]
    backward_span = backward_reach[:, 0][:, None] * backward_kept[0][None, :]
    forward_inflow = inflow[:half_count]
    backward_inflow = inflow[half_count:]
    current = distribution
    for sweep_index in range(SWEEPS):
        moment_field = summed_moments(current, weighted_rows)
        source = jnp.dot(
            source_rows.T, moment_field, precision=PRECISE, preferred_element_type=jnp.float32
        )
        source = source.reshape(2, velocity_count // (2 * classes), classes, cells_x, cells_y)
        relaxed = jnp.einsum("kyz,srkxz->srkxy", operator, source, precision=PRECISE)
        relaxed = relaxed.reshape(velocity_count, cells_x, cells_y)
        forward_local, forward_end = local_march(
            relaxed[:half_count], forward_rates, retained, False
        )
        backward_local, backward_end = local_march(
            relaxed[half_count:], backward_rates, retained, True
        )
        forward_in = forward_inflow
        backward_in = backward_inflow
        for segment in range(sections - 1):
            forward_out = forward_span * forward_in + forward_end
            backward_out = backward_span * backward_in + backward_end
            arrived_forward = from_behind(forward_out, "gx", 1)
            arrived_backward = from_behind(backward_out, "gx", -1)
            forward_in = jnp.where(section == 0, forward_inflow, arrived_forward)
            backward_in = jnp.where(section == sections - 1, backward_inflow, arrived_backward)
        forward_field = (
            forward_local
            + forward_reach[:, :, None] * forward_kept[None, :, :] * forward_in[:, None, :]
        )
        backward_field = (
            backward_local
            + backward_reach[:, :, None] * backward_kept[None, :, :] * backward_in[:, None, :]
        )
        current = jnp.concatenate([forward_field, backward_field], axis=0)
    final_moments = summed_moments(current, weighted_rows)
    return (current, final_moments.reshape(8, cells_x, cells_y))


def solution(mesh):
    in_specs = (
        P("vel", "gx", None),
        P(None, "vel"),
        P("vel"),
        P("vel"),
        P(),
        P("vel", None),
        P("gx", None),
    )
    out_specs = (P("vel", "gx", None), P(None, "gx", None))
    return jax.shard_map(
        per_device, mesh=mesh, in_specs=in_specs, out_specs=out_specs, check_vma=False
    )
```

profile of v0, /device:TPU:1, one launch (start us, length us, event | category | flops | bytes accessed | tf_op | source)
XLA Modules:
  0.0 636.4 jit_solution(11201019196031347092)
XLA Ops:
  8.8 5.4 fusion
  16.3 136.9 %all-reduce.4.cloned.1.call-done = f32[8,2048]{1,0:T(8,128)} async-done(((f32[8,2048]{1,0:T(8,128)}), f32[8,2048]{1,0:T(8,128)}) %all-reduce.4.cloned.1.call-update) | async-done | bytes 65552 | tf_op jit(solution)/shard_map/psum | solution.py:66
  153.2 3.8 convolution_bitcast_fusion.1
  157.7 3.6 fusion.15
  166.5 7.7 %collective-permute-start = (f32[216,128]{1,0:T(8,128)S(1)}, f32[216,128]{1,0:T(8,128)S(1)}, u32[]{:S(2)}, u32[]{:S(2)}) collective-permute-start(f32[216,128]{1,0:T(8,128)S(1)} %get-tuple-element.46), channel_id=1, source_target_pairs={{0,1},{1,2},{2,3},{3,4},{4,5},{5,6},{6,7},{8,9},{9,10},{10,11},{11... | collective-permute-start | bytes 331784 | tf_op jit(solution)/shard_map/ppermute | solution.py:18
  174.6 2.1 collective-permute-start.7
  177.1 3.6 collective-permute-start.1
  182.6 4.3 collective-permute-start.2
  188.8 4.3 collective-permute-start.3
  195.0 4.3 collective-permute-start.4
  201.2 4.3 collective-permute-start.5
  207.3 4.3 collective-permute-start.6
  213.5 1.9 collective-permute-start.8
  215.6 4.7 collective-permute-done.8
  220.3 1.9 collective-permute-start.9
  222.3 4.1 collective-permute-done.9
  226.5 1.9 collective-permute-start.10
  228.6 3.9 collective-permute-done.10
  232.7 1.9 collective-permute-start.11
  234.7 4.0 collective-permute-done.11
  238.9 1.9 collective-permute-start.12
  240.8 4.1 collective-permute-done.12
  245.0 1.9 collective-permute-start.13
  247.1 3.9 collective-permute-done.13
  252.4 3.7 fusion.23
  256.1 2.4 fusion.3
  259.0 132.3 %all-reduce.6.cloned.1.call-done = f32[8,2048]{1,0:T(8,128)} async-done(((f32[8,2048]{1,0:T(8,128)}), f32[8,2048]{1,0:T(8,128)}) %all-reduce.6.cloned.1.call-update) | async-done | bytes 65552 | tf_op jit(solution)/shard_map/psum | solution.py:66
  391.3 3.8 convolution_bitcast_fusion
  396.2 3.6 fusion.18
  401.9 7.7 %collective-permute-start.14 = (f32[216,128]{1,0:T(8,128)S(1)}, f32[216,128]{1,0:T(8,128)S(1)}, u32[]{:S(2)}, u32[]{:S(2)}) collective-permute-start(f32[216,128]{1,0:T(8,128)S(1)} %get-tuple-element.6), channel_id=1, source_target_pairs={{0,1},{1,2},{2,3},{3,4},{4,5},{5,6},{6,7},{8,9},{9,10},{10,11},{11... | collective-permute-start | bytes 331784 | tf_op jit(solution)/shard_map/ppermute | solution.py:18
  411.3 1.9 collective-permute-start.21
  415.3 3.8 collective-permute-start.15
  420.8 4.3 collective-permute-start.16
  427.0 4.3 collective-permute-start.17
  433.2 4.3 collective-permute-start.18
  439.3 4.3 collective-permute-start.19
  445.5 4.3 collective-permute-start.20
  451.7 1.9 collective-permute-start.22
  453.8 4.6 collective-permute-done.22
  460.6 4.0 collective-permute-done.23
  464.7 1.9 collective-permute-start.24
  466.7 4.1 collective-permute-done.24
  473.0 3.9 collective-permute-done.25
  480.8 2.3 collective-permute-done.26
  483.2 1.9 collective-permute-start.27
  486.9 2.4 collective-permute-done.27
  495.7 2.9 copy.202
  498.6 129.6 %all-reduce.8.cloned.1.call-done = f32[8,16,128]{2,1,0:T(8,128)} async-done(((f32[8,16,128]{2,1,0:T(8,128)}), f32[8,16,128]{2,1,0:T(8,128)}) %all-reduce.8.cloned.1.call-update) | async-done | bytes 65552 | tf_op jit(solution)/shard_map/psum | solution.py:66
  (177 shorter events, 59.0 us)
Async XLA Ops:
  7.2 146.0 %all-reduce.4.cloned.1.call-start = ((), (), s32[]{:S(2)}) async-start(), calls=%async_computation | async-start | bytes 131072 | tf_op jit(solution)/shard_map/psum | solution.py:66
  8.8 5.7 copy-start.8
  8.8 6.3 copy-start.5
  14.2 377.0 %all-reduce.6.cloned.1.call-start = ((), (), s32[]{:S(2)}) async-start(), calls=%async_computation.1 | async-start | bytes 131072 | tf_op jit(solution)/shard_map/psum | solution.py:66
  16.2 141.5 %copy-start.6 = (f32[12,128,128]{2,1,0:T(8,128)}, f32[12,128,128]{2,1,0:T(8,128)S(1)}, u32[]{:S(2)}) copy-start(f32[12,128,128]{2,1,0:T(8,128)S(1)} %rev.9) | copy-start | bytes 2359300
  165.2 0.9 copy-start
  166.5 10.5 %collective-permute-start = (f32[216,128]{1,0:T(8,128)S(1)}, f32[216,128]{1,0:T(8,128)S(1)}, u32[]{:S(2)}, u32[]{:S(2)}) collective-permute-start(f32[216,128]{1,0:T(8,128)S(1)} %get-tuple-element.46), channel_id=1, source_target_pairs={{0,1},{1,2},{2,3},{3,4},{4,5},{5,6},{6,7},{8,9},{9,10},{10,11},{11... | collective-permute-start | bytes 331784 | tf_op jit(solution)/shard_map/ppermute | solution.py:18
  174.6 37.3 %collective-permute-start.7 = (f32[216,128]{1,0:T(8,128)S(1)}, f32[216,128]{1,0:T(8,128)S(1)}, u32[]{:S(2)}, u32[]{:S(2)}) collective-permute-start(f32[216,128]{1,0:T(8,128)S(1)} %get-tuple-element.56), channel_id=1, source_target_pairs={{1,0},{2,1},{3,2},{4,3},{5,4},{6,5},{7,6},{9,8},{10,9},{11,10},{12... | collective-permute-start | bytes 331784 | tf_op jit(solution)/shard_map/ppermute | solution.py:18
  177.1 5.4 collective-permute-start.1
  182.6 6.1 collective-permute-start.2
  188.8 6.1 collective-permute-start.3
  195.0 6.1 collective-permute-start.4
  201.2 6.1 collective-permute-start.5
  207.3 6.1 collective-permute-start.6
  213.5 6.8 %collective-permute-start.8 = (f32[216,128]{1,0:T(8,128)S(1)}, f32[216,128]{1,0:T(8,128)S(1)}, u32[]{:S(2)}, u32[]{:S(2)}) collective-permute-start(f32[216,128]{1,0:T(8,128)S(1)} %get-tuple-element.134), channel_id=1, source_target_pairs={{1,0},{2,1},{3,2},{4,3},{5,4},{6,5},{7,6},{9,8},{10,9},{11,10},{12... | collective-permute-start | bytes 331784 | tf_op jit(solution)/shard_map/ppermute | solution.py:18
  220.3 6.1 collective-permute-start.9
  226.5 6.1 collective-permute-start.10
  232.7 6.1 collective-permute-start.11
  238.9 6.1 collective-permute-start.12
  245.0 6.1 collective-permute-start.13
  251.9 4.2 copy-start.1
  252.4 3.7 copy-start.9
  258.5 369.7 %all-reduce.8.cloned.1.call-start = ((), (), s32[]{:S(2)}) async-start(), calls=%async_computation.2 | async-start | bytes 131072 | tf_op jit(solution)/shard_map/psum | solution.py:66
  395.1 1.1 copy-start.7
  401.9 13.3 %collective-permute-start.14 = (f32[216,128]{1,0:T(8,128)S(1)}, f32[216,128]{1,0:T(8,128)S(1)}, u32[]{:S(2)}, u32[]{:S(2)}) collective-permute-start(f32[216,128]{1,0:T(8,128)S(1)} %get-tuple-element.6), channel_id=1, source_target_pairs={{0,1},{1,2},{2,3},{3,4},{4,5},{5,6},{6,7},{8,9},{9,10},{10,11},{11... | collective-permute-start | bytes 331784 | tf_op jit(solution)/shard_map/ppermute | solution.py:18
  411.3 38.5 %collective-permute-start.21 = (f32[216,128]{1,0:T(8,128)S(1)}, f32[216,128]{1,0:T(8,128)S(1)}, u32[]{:S(2)}, u32[]{:S(2)}) collective-permute-start(f32[216,128]{1,0:T(8,128)S(1)} %get-tuple-element.22), channel_id=1, source_target_pairs={{1,0},{2,1},{3,2},{4,3},{5,4},{6,5},{7,6},{9,8},{10,9},{11,10},{12... | collective-permute-start | bytes 331784 | tf_op jit(solution)/shard_map/ppermute | solution.py:18
  415.3 5.4 collective-permute-start.15
  420.8 6.1 collective-permute-start.16
  427.0 6.1 collective-permute-start.17
  433.2 6.1 collective-permute-start.18
  439.3 6.1 collective-permute-start.19
  445.5 6.1 collective-permute-start.20
  451.7 6.8 %collective-permute-start.22 = (f32[216,128]{1,0:T(8,128)S(1)}, f32[216,128]{1,0:T(8,128)S(1)}, u32[]{:S(2)}, u32[]{:S(2)}) collective-permute-start(f32[216,128]{1,0:T(8,128)S(1)} %get-tuple-element.132), channel_id=1, source_target_pairs={{1,0},{2,1},{3,2},{4,3},{5,4},{6,5},{7,6},{9,8},{10,9},{11,10},{12... | collective-permute-start | bytes 331784 | tf_op jit(solution)/shard_map/ppermute | solution.py:18
  458.5 6.1 collective-permute-start.23
  464.7 6.1 collective-permute-start.24
  466.7 12.4 %copy-start.2 = (f32[216,16,128]{2,1,0:T(8,128)S(1)}, f32[216,16,128]{2,1,0:T(8,128)}, u32[]{:S(2)}) copy-start(f32[216,16,128]{2,1,0:T(8,128)} %copy-done.1) | copy-start | bytes 5308420
  470.9 6.1 collective-permute-start.25
  477.1 6.1 collective-permute-start.26
  483.2 6.1 collective-permute-start.27
  491.2 1.8 copy-start.10
  493.0 2.5 copy-start.3
  493.0 2.5 copy-start.4
Sparse Core Ops, SparseCore 0:
  14.4 138.7 all-reduce.3
  258.7 132.5 all-reduce.5
  495.6 132.6 all-reduce.7
where the time goes:
time: 643 us; the launch traced here: 636 us
  waiting for transfers between devices  464 us (72%)
  starting transfers between devices  93.9 us (15%)
  matrix products  24.4 us (4%)
  other arithmetic  21.6 us (3%)
  local copies, waits for them, and re-layouts  16.4 us (3%)
  between operations  15.8 us (2%)
    psum x3, waiting for transfers between devices, summed_moments(): return lax.psum(partial_sum, 'vel')  399 us
    ppermute x28, starting transfers between devices, from_behind(): return lax.ppermute(block, axis, route)  93.2 us
    ppermute x28, waiting for transfers between devices, from_behind(): return lax.ppermute(block, axis, route)  65.4 us
  transfers between devices with their start and end apart: 31, of which 27 were waited for; matrix products, arithmetic and copies ran while one was open for 3% of the time, Pallas kernels for 0%

commit v1 on v0

v1 whole, which is shorter than its diff:
```python
import functools

import jax
import jax.numpy as jnp
from jax import lax
from jax.experimental import pallas as pl
from jax.experimental.pallas import tpu as pltpu
from jax.sharding import PartitionSpec as P


SHAKHOV = 4.0 / 45.0
KNUDSEN_STEP = 0.004
ABSORB = 0.3
SWEEPS = 2
MESH = pl.DeviceIdType.MESH
F32 = jnp.float32
BF16 = jnp.bfloat16

V = 432
H = 216
HP = 224
NC = 12
NM = 8
XS = 16
T = 32
PLANE = 32
CHIPS = 4


def split(x):
    hi = x.astype(BF16)
    return hi, (x - hi.astype(F32)).astype(BF16)


def dot(a, b):
    return jnp.dot(a, b, preferred_element_type=F32)


def rows_of(ax, ay, az, sx, sy, sz):
    cx, cy, cz = ax * sx, ay * sy, az * sz
    e = cx * cx + cy * cy + cz * cz
    f = e - 2.5
    one = jnp.ones_like(cx)
    phi = [one, cx, cy, cz, e * (2.0 / 3.0) - 1.0, cx * f, cy * f, cz * f]
    psi = [one, 2.0 * cx, 2.0 * cy, 2.0 * cz, e - 1.5, SHAKHOV * cx * f, SHAKHOV * cy * f, SHAKHOV * cz * f]
    return phi, psi


def body(
    dist, speeds, weights, octant, inverses, inflow, solid,
    out_h, out_m,
    dx, spd, wall, wdir, inv, infl, sbuf, part0, part, own, rb1, rb2, mb, mo,
    b3, a3, at, abc, a32, ks, kc, kp, tsc, t2, gs, hloc, mloc, ebuf, esrc, hin,
    dsem, isem, ssend, srecv, rsend, rrecv, gsend, grecv, esend, erecv, osend, orecv, olocal,
):
    vel = lax.axis_index("vel")
    gx = lax.axis_index("gx")
    y = gx // 2
    c = gx % 2
    owner = (vel % 2) == c
    p = jnp.where(c == 0, y, CHIPS - 1 - y)

    def step_of(row, core):
        return jnp.where(core == 0, row, T - 1 - row)

    def remote(src, dst, ss, rs, tv, tg):
        return pltpu.make_async_remote_copy(
            src_ref=src, dst_ref=dst, send_sem=ss, recv_sem=rs, device_id=(tv, tg), device_id_type=MESH
        )

    def send(src, dst, ss, rs, tv, tg):
        here = (tv == vel) & (tg == gx)

        @pl.when(here)
        def _():
            pltpu.make_async_copy(src, dst, rs).start()

        @pl.when(jnp.logical_not(here))
        def _():
            remote(src, dst, ss, rs, tv, tg).start()

    for x in range(XS):
        pltpu.make_async_copy(dist.at[:, x, :], dx.at[x], dsem.at[x]).start()
    inv_copy = pltpu.make_async_copy(inverses, inv, isem.at[0])
    inv_copy.start()
    infl_copy = pltpu.make_async_copy(
        inflow.at[pl.ds(pl.multiple_of(c * H, 8), H)], infl.at[pl.ds(0, H)], isem.at[1]
    )
    infl_copy.start()

    barrier = pltpu.get_barrier_semaphore()

    def greet(i, _):
        tv, tg = i // 2, 2 * y + i % 2

        @pl.when(jnp.logical_not((tv == vel) & (tg == gx)))
        def _():
            pl.semaphore_signal(barrier, inc=1, device_id=(tv, tg), device_id_type=MESH)

        return 0

    lax.fori_loop(0, 2 * PLANE, greet, 0)
    for o in range(1, CHIPS):
        for cc in range(2):
            pl.semaphore_signal(
                barrier, inc=1, device_id=(vel, lax.rem(y + o, CHIPS) * 2 + cc), device_id_type=MESH
            )

    lane = lax.broadcasted_iota(jnp.int32, (1, 512), 1)
    quadrant = octant[0]
    sy = (1 - 2 * lax.rem(quadrant, 2)).astype(F32)
    sz = (1 - 2 * lax.div(quadrant, 2)).astype(F32)
    spd[...] = jnp.zeros_like(spd)
    spd[0:3, 0:V] = speeds[...]
    spd[3:4, 0:V] = weights[...]
    sp = spd[...]
    sx_all = jnp.where(lane < H, 1.0, -1.0).astype(F32)
    phi, _ = rows_of(sp[0:1], sp[1:2], sp[2:3], sx_all, sy, sz)
    for m in range(NM):
        spd[m : m + 1, :] = phi[m] * sp[3:4]
    hi, lo = split(spd[...])
    wall[...] = jnp.concatenate([hi.astype(F32), lo.astype(F32)], axis=0).astype(BF16)

    for x in range(XS):
        pltpu.make_async_copy(dist.at[:, x, :], dx.at[x], dsem.at[x]).wait()
        hi, lo = split(dx[x])
        r = dot(wall[:, 0:V], jnp.concatenate([hi, lo], axis=1))
        part0[x] = r[0:8, 0:128] + r[8:16, 0:128] + r[0:8, 128:256] + r[8:16, 128:256]

    pl.semaphore_wait(barrier, 2 * PLANE - 1 + 2 * (CHIPS - 1))

    def rs1(i, _):
        i = lax.rem(i + vel, XS)
        row = XS * c + i
        send(part0.at[i], rb1.at[vel], rsend.at[0], rrecv.at[0], row, 2 * y + row % 2)
        return 0

    lax.fori_loop(0, XS, rs1, 0)

    for o in range(1, 2 * CHIPS):
        remote(solid, sbuf.at[gx], ssend, srecv, vel, lax.rem(gx + o, 2 * CHIPS)).start()
    pltpu.make_async_copy(solid, sbuf.at[gx], srecv).start()

    sp = jnp.where(c == 0, sp, pltpu.roll(sp, 512 - H, 1))
    sp = jnp.where(lane < H, sp, 0.0)
    sp = sp[:, 0:256]
    live = (lane < H).astype(F32)[:, 0:256]
    sx = (1 - 2 * c).astype(F32)
    phi, psi = rows_of(sp[0:1], sp[1:2], sp[2:3], sx, sy, sz)
    rate = sp[0:1] / (sp[0:1] + KNUDSEN_STEP)
    for m in range(NM):
        spd[m : m + 1, 0:256] = phi[m] * sp[3:4]
        spd[m : m + 1, 256:512] = psi[m] * ((1.0 - rate) * live)
    wd = spd[:, 0:256]
    ps = spd[:, 256:512]
    hi, lo = split(wd)
    wdir[...] = jnp.concatenate([hi.astype(F32), lo.astype(F32)], axis=0).astype(BF16)
    cls = lax.rem(lax.broadcasted_iota(jnp.int32, (8, 256), 1), NC)
    hi, lo = split(ps)
    hi, lo = hi.astype(F32), lo.astype(F32)
    for k in range(NC):
        at[8 * k : 8 * k + 8] = jnp.where(cls == k, hi, 0.0)
        at[96 + 8 * k : 104 + 8 * k] = jnp.where(cls == k, lo, 0.0)
        at[192 + 8 * k : 200 + 8 * k] = jnp.where(cls == k, hi, 0.0)
    at[288:384] = jnp.zeros((96, 256), F32)
    a3[...] = at[...].T[0:HP].astype(BF16)
    abc[...] = jnp.broadcast_to(rate, (128, 256)).T[0:HP]
    pw = abc[...]
    for _ in range(5):
        pw = pw * pw
    a32[...] = pw
    infl[H:HP] = jnp.zeros((HP - H, 128), F32)
    infl_copy.wait()

    def powers(t, cur):
        cur = cur * rate
        tsc[t] = cur
        return cur

    lax.fori_loop(0, T, powers, wd)
    hi, lo = split(tsc[...].reshape(T * NM, 256))
    t2[0 : T * NM] = hi
    t2[T * NM : 2 * T * NM] = lo

    def gather(rb, n, k, wait):
        @pl.when(owner)
        def _():
            full = rb.at[pl.ds(0, n)]
            remote(full, full, rsend.at[k], rrecv.at[k], vel, gx).wait_recv()
            own[k] = jnp.sum(rb[...].reshape(n // 8, 8, NM, 128), axis=0).sum(axis=0)

    gather(rb1, PLANE, 0, None)

    def spread(k, dst):
        @pl.when(owner)
        def _():
            def one(i, _):
                j = lax.rem(i + 2 * vel + c + 1, 2 * PLANE)
                tv, tc = j // 2, j % 2
                send(own.at[k], dst.at[step_of(vel, tc)], gsend.at[k], grecv.at[k], tv, 2 * y + tc)
                return 0

            lax.fori_loop(0, 2 * PLANE, one, 0)

    spread(0, mb.at[0])

    inv_copy.wait()
    ii = lax.broadcasted_iota(jnp.int32, (128, 128), 0)
    jj = lax.broadcasted_iota(jnp.int32, (128, 128), 1)
    perm = (ii == jnp.where(lax.rem(quadrant, 2) == 0, jj, 127 - jj)).astype(F32).astype(BF16)
    for n in range(NC // 2):
        parts = split(inv[2 * n : 2 * n + 2].reshape(256, 128))
        for q, w in enumerate(parts):
            u = lax.dot_general(perm, w, (((1,), (1,)), ((), ())), preferred_element_type=F32)
            u = jnp.concatenate([u[:, 0:128], u[:, 128:256]], axis=0).astype(BF16)
            v = dot(u, perm).astype(BF16)
            v = jnp.concatenate([v[0:128], v[128:256]], axis=1)
            cols = slice(256 * n, 256 * n + 256)
            if q == 0:
                b3[0:128, cols] = v
                b3[128:256, cols] = v
            else:
                b3[256:384, cols] = v

    remote(sbuf, sbuf, ssend, srecv, vel, gx).wait_recv()
    for chip in range(CHIPS):
        keep = 1.0 - ABSORB * sbuf[2 * chip : 2 * chip + 2].astype(F32).reshape(4, 8, 128)
        keep = (keep[0] * keep[1]) * (keep[2] * keep[3])
        for s in (4, 2, 1):
            keep = keep * pltpu.roll(keep, s, 0)
        kp[chip] = keep

    def cells(t, cur):
        x = step_of(t, c)
        keep = 1.0 - ABSORB * sbuf[2 * y + x // XS, pl.ds(x % XS, 1), :].astype(F32)
        keep = jnp.broadcast_to(keep, (8, 128))
        cur = cur * keep
        ks[t] = keep
        kc[t] = cur
        return cur

    lax.fori_loop(0, T, cells, jnp.ones((8, 128), F32))

    for s in range(SWEEPS):
        remote(mb.at[s], mb.at[s], gsend.at[s], grecv.at[s], vel, gx).wait_recv()
        hi, lo = split(mb[s].reshape(T * NM, 128))
        l3 = jnp.concatenate([hi, lo, hi], axis=1)
        for n in range(NC // 2):
            g = dot(l3, b3[:, 256 * n : 256 * n + 256]).reshape(T, NM, 256)
            hi, lo = split(jnp.concatenate([g[:, :, 0:128], g[:, :, 128:256]], axis=1))
            gs[:, 16 * n : 16 * n + 16, :] = hi
            gs[:, 96 + 16 * n : 112 + 16 * n, :] = hi
            gs[:, 192 + 16 * n : 208 + 16 * n, :] = lo

        def march(u, h):
            t = 2 * u
            r = dot(a3[:, 0:288], jnp.concatenate([gs[t], gs[t + 1]], axis=1))
            a = abc[...].reshape(HP // 8, 8, 128)
            for d in range(2):
                h = h * (a * ks[t + d][None]) + r[:, 128 * d : 128 * d + 128].reshape(HP // 8, 8, 128)
                hloc[t + d] = h.reshape(HP, 128)
            return h

        h = lax.fori_loop(0, T // 2, march, jnp.zeros((HP // 8, 8, 128), F32), unroll=2)
        esrc[s] = h.reshape(HP, 128)

        for q in (3, 2, 1):

            @pl.when(q > p)
            def _():
                ty = jnp.where(c == 0, q, CHIPS - 1 - q)
                remote(esrc.at[s], ebuf.at[s, p], esend.at[s, q - 1], erecv.at[s, p], vel, 2 * ty + c).start()

        def local_moments(u, _):
            t = 2 * u
            hi, lo = split(jnp.concatenate([hloc[t], hloc[t + 1]], axis=1))
            r = dot(wdir[:, 0:HP], hi) + dot(wdir[:, 0:HP], lo)
            r = r[0:8] + r[8:16]
            mloc[t] = r[:, 0:128]
            mloc[t + 1] = r[:, 128:256]
            return 0

        lax.fori_loop(0, T // 2, local_moments, 0, unroll=2)

        hin[...] = infl[...]
        for q in range(CHIPS - 1):

            @pl.when(q < p)
            def _():
                remote(esrc.at[s], ebuf.at[s, q], esend.at[s, 0], erecv.at[s, q], vel, gx).wait_recv()
                k = kp[jnp.where(c == 0, q, CHIPS - 1 - q)]
                span = a32[...].reshape(HP // 8, 8, 128) * k[None]
                now = hin[...].reshape(HP // 8, 8, 128) * span + ebuf[s, q].reshape(HP // 8, 8, 128)
                hin[...] = now.reshape(HP, 128)

        hi, lo = split(hin[...])
        r = dot(t2[:, 0:HP], jnp.concatenate([hi, lo], axis=1))
        n = T * NM
        r = (r[0:n, 0:128] + r[n : 2 * n, 0:128]) + (r[0:n, 128:256] + r[n : 2 * n, 128:256])
        part[s] = mloc[...] + kc[...] * r.reshape(T, NM, 128)

        def rs(i, _):
            row = lax.rem(i + vel, T)
            send(
                part.at[s, step_of(row, c)], rb2.at[s, 2 * vel + c], rsend.at[s + 1], rrecv.at[s + 1],
                row, 2 * y + row % 2,
            )
            return 0

        lax.fori_loop(0, T, rs, 0)

        if s == SWEEPS - 1:
            def finish(t, h):
                a = abc[...].reshape(HP // 8, 8, 128)
                h = h * (a * ks[t][None])
                hloc[t] = (hloc[t].reshape(HP // 8, 8, 128) + h).reshape(HP, 128)
                return h

            first = pl.multiple_of(c * H, 8)

            def far(t, h):
                h = finish(t, h)
                x = jnp.where(c == 0, t - XS, T - 1 - t)
                remote(
                    hloc.at[t, pl.ds(0, H)], out_h.at[pl.ds(first, H), x, :], osend, orecv, vel, 2 * y + 1 - c
                ).start()
                return h

            def near(t, h):
                h = finish(t, h)
                x = jnp.where(c == 0, t, XS - 1 - t)
                pltpu.make_async_copy(hloc.at[t, pl.ds(0, H)], out_h.at[pl.ds(first, H), x, :], olocal).start()
                return h

            h = lax.fori_loop(0, XS, near, hin[...].reshape(HP // 8, 8, 128))
            lax.fori_loop(XS, T, far, h)

        gather(rb2.at[s], 2 * PLANE, s + 1, None)
        if s < SWEEPS - 1:
            spread(s + 1, mb.at[s + 1])

    last = SWEEPS
    section = vel // XS

    @pl.when(owner)
    def _():
        def one(i, _):
            tv = lax.rem(i + vel + 1, PLANE)
            send(own.at[last], mo.at[vel % XS], gsend.at[last], grecv.at[last], tv, 2 * y + section)
            return 0

        lax.fori_loop(0, PLANE, one, 0)

    remote(mo, mo, gsend.at[last], grecv.at[last], vel, gx).wait_recv()
    for x in range(XS):
        out_m[:, x, :] = mo[x]

    for o in range(1, 2 * CHIPS):
        remote(solid, sbuf.at[gx], ssend, srecv, vel, gx).wait_send()
    mine = owner & (section == c)

    def drain(buf, n, less, sem):
        @pl.when(less)
        def _():
            remote(buf.at[pl.ds(0, n - 1)], buf.at[pl.ds(0, n - 1)], sem, sem, vel, gx).wait_send()

        @pl.when(jnp.logical_not(less))
        def _():
            remote(buf.at[pl.ds(0, n)], buf.at[pl.ds(0, n)], sem, sem, vel, gx).wait_send()

    drain(part0, XS, mine, rsend.at[0])
    for s in range(SWEEPS):
        drain(part.at[s], T, owner, rsend.at[s + 1])
        for q in (3, 2, 1):

            @pl.when(q > p)
            def _():
                remote(esrc.at[s], esrc.at[s], esend.at[s, q - 1], esend.at[s, q - 1], vel, gx).wait_send()

    @pl.when(owner)
    def _():
        for k in range(SWEEPS):
            few = rb2.at[0, pl.ds(0, 2 * PLANE - 1)]
            remote(few, few, gsend.at[k], gsend.at[k], vel, gx).wait_send()
        drain(rb2.at[0], PLANE, section == c, gsend.at[last])

    half = hloc.at[pl.ds(0, XS), pl.ds(0, H)]
    remote(half, half, osend, orecv, vel, gx).wait()
    pltpu.make_async_copy(half, half, olocal).wait()


def per_device(distribution, speeds, weights, octant, inverses, inflow, solid_cells):
    dma = pltpu.SemaphoreType.DMA
    vm = pltpu.VMEM
    scratch = [
        vm((XS, V, 128), F32), vm((8, 512), F32), vm((16, 512), BF16), vm((16, 256), BF16),
        vm((NC, 128, 128), F32), vm((HP, 128), F32), vm((2 * CHIPS, XS, 128), jnp.int32),
        vm((XS, NM, 128), F32), vm((SWEEPS, T, NM, 128), F32), vm((SWEEPS + 1, NM, 128), F32),
        vm((PLANE, NM, 128), F32), vm((SWEEPS, 2 * PLANE, NM, 128), F32), vm((SWEEPS, T, NM, 128), F32),
        vm((XS, NM, 128), F32),
        vm((384, NC * 128), BF16), vm((HP, 384), BF16), vm((384, 256), F32), vm((HP, 128), F32),
        vm((HP, 128), F32), vm((T, 8, 128), F32), vm((T, 8, 128), F32), vm((CHIPS, 8, 128), F32),
        vm((T, 8, 256), F32), vm((2 * T * NM, 256), BF16), vm((T, 288, 128), BF16), vm((T, HP, 128), F32),
        vm((T, NM, 128), F32), vm((SWEEPS, CHIPS - 1, HP, 128), F32), vm((SWEEPS, HP, 128), F32),
        vm((HP, 128), F32),
        dma((XS,)), dma((2,)), dma, dma, dma((SWEEPS + 1,)), dma((SWEEPS + 1,)), dma((SWEEPS + 1,)),
        dma((SWEEPS + 1,)), dma((SWEEPS, CHIPS - 1)), dma((SWEEPS, CHIPS - 1)), dma, dma, dma,
    ]
    hbm = pl.BlockSpec(memory_space=pl.ANY)
    vmem = pl.BlockSpec(memory_space=pltpu.VMEM)
    return pl.pallas_call(
        body,
        out_shape=(
            jax.ShapeDtypeStruct((V, XS, 128), F32),
            jax.ShapeDtypeStruct((NM, XS, 128), F32),
        ),
        in_specs=[hbm, vmem, vmem, pl.BlockSpec(memory_space=pltpu.SMEM), hbm, hbm, hbm],
        out_specs=(hbm, vmem),
        scratch_shapes=scratch,
        name="solve",
        compiler_params=pltpu.CompilerParams(
            collective_id=0, has_side_effects=True, vmem_limit_bytes=48 * 2**20
        ),
    )(distribution, speeds, weights.reshape(1, V), octant, inverses, inflow, solid_cells)


def solution(mesh):
    in_specs = (
        P("vel", "gx", None),
        P(None, "vel"),
        P("vel"),
        P("vel"),
        P(),
        P("vel", None),
        P("gx", None),
    )
    out_specs = (P("vel", "gx", None), P(None, "gx", None))
    return jax.shard_map(
        per_device, mesh=mesh, in_specs=in_specs, out_specs=out_specs, check_vma=False
    )
```

time: 643 us -> 76.3 us (0.12)
  waiting for transfers between devices: 464 us -> 0 us
  starting transfers between devices: 93.9 us -> 0 us
  Pallas kernels: 0 us -> 68.2 us
  matrix products: 24.4 us -> 0 us
  other arithmetic: 21.6 us -> 0 us
  between operations: 15.8 us -> 1.3 us
  local copies, waits for them, and re-layouts: 16.4 us -> 6.56 us
    psum x3 -> x0, waiting for transfers between devices: 399 us -> none  [summed_moments(): return lax.psum(partial_sum, 'vel')]
    ppermute x28 -> x0, starting transfers between devices: 93.2 us -> none  [from_behind(): return lax.ppermute(block, axis, route)]
    pallas_call x0 -> x1, Pallas kernels: none -> 68.2 us  [per_device(): pl.pallas_call(body, out_shape=(jax.ShapeDtypeStruct((V, XS, 128), F32),...]
    ppermute x28 -> x0, waiting for transfers between devices: 65.4 us -> none  [from_behind(): return lax.ppermute(block, axis, route)]
    dot_general x7 -> x0, matrix products: 24.4 us -> none  [the longest x3 9.57 us: summed_moments(): jnp.dot(weighted_rows, flattened, precision=PRECISE, preferred_element_ty...]
    add x31 -> x0, other arithmetic: 14.3 us -> none  [the longest x3 7.2 us: per_device(): backward_local + backward_reach[:, :, None] * backward_kept[None, :, :] *...]
  transfers between devices with their start and end apart: 31 -> 0, of which waited for: 27 -> 0; matrix products, arithmetic and copies ran while one was open for 3% -> 0% of each run, Pallas kernels for 0% -> 0%
where the time goes in v1:
time: 76.3 us; the launch traced here: 76.1 us
  Pallas kernels  68.2 us (89%)
  local copies, waits for them, and re-layouts  6.56 us (9%)
  between operations  1.3 us (2%)
    pallas_call x1, Pallas kernels, per_device(): pl.pallas_call(body, out_shape=(jax.ShapeDtypeStruct((V, XS, 128), F32),...  68.2 us
    unnamed x12, local copies, waits for them, and re-layouts  6.56 us

profile of v1, /device:TPU:1, one launch (start us, length us, event | category | flops | bytes accessed | tf_op | source)
XLA Modules:
  0.0 76.1 jit_solution(14767584360437683467)
XLA Ops:
  1.3 0.0 copy-start
  1.3 1.1 %copy-done = f32[12,128,128]{2,1,0:T(8,128)S(1)} copy-done((f32[12,128,128]{2,1,0:T(8,128)S(1)}, f32[12,128,128]{2,1,0:T(8,128)}, u32[]{:S(2)}) %copy-start) | copy-done | bytes 786456
  2.4 0.0 copy-start.1
  2.4 0.9 %copy-done.1 = f32[432,128]{1,0:T(8,128)S(1)} copy-done((f32[432,128]{1,0:T(8,128)S(1)}, f32[432,128]{1,0:T(8,128)}, u32[]{:S(2)}) %copy-start.1) | copy-done | bytes 221208
  3.3 0.0 copy-start.2
  3.4 0.7 copy-done.2
  4.0 0.0 copy-start.3
  4.0 0.7 copy-done.3
  4.7 0.0 copy-start.4
  4.7 0.7 copy-done.4
  5.4 68.2 %solve.1 = (f32[432,16,128]{2,1,0:T(8,128)S(1)}, f32[8,16,128]{2,1,0:T(8,128)S(1)}) custom-call(f32[432,16,128]{2,1,0:T(8,128)} %dist.1, f32[3,432]{1,0:T(4,128)S(1)} %copy-done.2, f32[1,432]{1,0:T(1,128)S(1)} %bitcast.1, s32[1]{0:T(128)S(6)} %copy.11.octant, f32[12,128,128]{2,1,0:T(8,128)S(1)} %copy-done, f32[432,128]{1,0:T(8,128)S(1)} %copy-done.1, ...), custom_call_target="tpu_custom_call" | custom-call | tf_op jit(solution)/shard_map/solve/pallas_call | solution.py:411
  73.7 1.8 %copy.12 = f32[432,16,128]{2,1,0:T(8,128)} copy(f32[432,16,128]{2,1,0:T(8,128)S(1)} %get-tuple-element.4) | data formatting | bytes 7077888
  75.5 0.6 copy.13
Async XLA Ops:
  1.3 1.1 %copy-start = (f32[12,128,128]{2,1,0:T(8,128)S(1)}, f32[12,128,128]{2,1,0:T(8,128)}, u32[]{:S(2)}) copy-start(f32[12,128,128]{2,1,0:T(8,128)} %inverses.1) | copy-start | bytes 2359300
  2.4 0.9 %copy-start.1 = (f32[432,128]{1,0:T(8,128)S(1)}, f32[432,128]{1,0:T(8,128)}, u32[]{:S(2)}) copy-start(f32[432,128]{1,0:T(8,128)} %inflow.1) | copy-start | bytes 663556
  3.3 0.7 copy-start.2
  4.0 0.7 copy-start.3
  4.7 0.7 copy-start.4

commit v2 on v1

--- a/solution.py
+++ b/solution.py
@@ -24,6 +24,8 @@
 XS = 16
 T = 32
 PLANE = 32
+ZX = 4
+ZS = 8
 CHIPS = 4
 
 
@@ -47,16 +49,18 @@
 
 
 def body(
-    dist, speeds, weights, octant, inverses, inflow, solid,
+    dist, speeds_in, weights_in, octant, inverses, inflow, solid,
     out_h, out_m,
-    dx, spd, wall, wdir, inv, infl, sbuf, part0, part, own, rb1, rb2, mb, mo,
-    b3, a3, at, abc, a32, ks, kc, kp, tsc, t2, gs, hloc, mloc, ebuf, esrc, hin,
+    speeds, weights, dx, spd, wall, wdir, inv, infl, sbuf, part0, part, own, rb1, rb2, mb, mo,
+    b3, a3, at, abc, a32, ks, kc, kp, tsc, t2, gs, hloc, mloc, ebuf, esrc, hin, et, ec, kr,
     dsem, isem, ssend, srecv, rsend, rrecv, gsend, grecv, esend, erecv, osend, orecv, olocal,
 ):
     vel = lax.axis_index("vel")
     gx = lax.axis_index("gx")
     y = gx // 2
     c = gx % 2
+    xi = vel // ZS
+    zi = vel % ZS
     owner = (vel % 2) == c
     p = jnp.where(c == 0, y, CHIPS - 1 - y)
 
@@ -68,7 +72,10 @@
             src_ref=src, dst_ref=dst, send_sem=ss, recv_sem=rs, device_id=(tv, tg), device_id_type=MESH
         )
 
-    def send(src, dst, ss, rs, tv, tg):
+    def send(src, dst, ss, rs, tv, tg, maybe=True):
+        if not maybe:
+            remote(src, dst, ss, rs, tv, tg).start()
+            return
         here = (tv == vel) & (tg == gx)
 
         @pl.when(here)
@@ -79,6 +86,12 @@
         def _():
             remote(src, dst, ss, rs, tv, tg).start()
 
+    small = [
+        pltpu.make_async_copy(speeds_in, speeds, isem.at[2]),
+        pltpu.make_async_copy(weights_in, weights, isem.at[3]),
+    ]
+    for copy in small:
+        copy.start()
     for x in range(XS):
         pltpu.make_async_copy(dist.at[:, x, :], dx.at[x], dsem.at[x]).start()
     inv_copy = pltpu.make_async_copy(inverses, inv, isem.at[0])
@@ -90,16 +103,25 @@
 
     barrier = pltpu.get_barrier_semaphore()
 
+    def around(i):
+        return lax.rem(zi + ZS // 2 + ((i + 1) // 2) * (2 * (i % 2) - 1) + ZS, ZS)
+
     def greet(i, _):
-        tv, tg = i // 2, 2 * y + i % 2
-
-        @pl.when(jnp.logical_not((tv == vel) & (tg == gx)))
-        def _():
-            pl.semaphore_signal(barrier, inc=1, device_id=(tv, tg), device_id_type=MESH)
+        tz = around(i)
+        for o in (2, 1, 3, 0):
+            tv = lax.rem(xi + o, ZX) * ZS + tz
+            for cc in range(2):
+                if o:
+                    pl.semaphore_signal(barrier, inc=1, device_id=(tv, 2 * y + cc), device_id_type=MESH)
+                    continue
+
+                @pl.when(jnp.logical_not((tv == vel) & (cc == c)))
+                def _():
+                    pl.semaphore_signal(barrier, inc=1, device_id=(tv, 2 * y + cc), device_id_type=MESH)
 
         return 0
 
-    lax.fori_loop(0, 2 * PLANE, greet, 0)
+    lax.fori_loop(0, ZS, greet, 0)
     for o in range(1, CHIPS):
         for cc in range(2):
             pl.semaphore_signal(
@@ -107,6 +129,8 @@
             )
 
     lane = lax.broadcasted_iota(jnp.int32, (1, 512), 1)
+    for copy in small:
+        copy.wait()
     quadrant = octant[0]
     sy = (1 - 2 * lax.rem(quadrant, 2)).astype(F32)
     sz = (1 - 2 * lax.div(quadrant, 2)).astype(F32)
@@ -130,12 +154,13 @@
     pl.semaphore_wait(barrier, 2 * PLANE - 1 + 2 * (CHIPS - 1))
 
     def rs1(i, _):
-        i = lax.rem(i + vel, XS)
-        row = XS * c + i
-        send(part0.at[i], rb1.at[vel], rsend.at[0], rrecv.at[0], row, 2 * y + row % 2)
+        tz = around(i)
+        for o in range(2):
+            row = (2 * c + o) * ZS + tz
+            send(part0.at[o * ZS + tz], rb1.at[vel], rsend.at[0], rrecv.at[0], row, 2 * y + tz % 2)
         return 0
 
-    lax.fori_loop(0, XS, rs1, 0)
+    lax.fori_loop(0, ZS, rs1, 0)
 
     for o in range(1, 2 * CHIPS):
         remote(solid, sbuf.at[gx], ssend, srecv, vel, lax.rem(gx + o, 2 * CHIPS)).start()
@@ -182,6 +207,19 @@
     t2[0 : T * NM] = hi
     t2[T * NM : 2 * T * NM] = lo
 
+    def remains(t, cur):
+        tsc[T - 1 - t] = cur
+        return cur * rate
+
+    lax.fori_loop(0, T, remains, ps)
+    late = tsc[...].reshape(T * NM, 256).T
+    for d in range(2):
+        et[d, 0:256] = late[:, 128 * d : 128 * d + 128]
+        et[d, 256:288] = jnp.zeros((32, 128), F32)
+    for k in range(NC):
+        hi, lo = split(jnp.concatenate([et[d, pl.ds(k, 24, stride=NC), :] for d in range(2)], axis=1))
+        ec[k] = jnp.concatenate([hi.astype(F32), lo.astype(F32)], axis=0).astype(BF16)
+
     def gather(rb, n, k, wait):
         @pl.when(owner)
         def _():
@@ -195,12 +233,15 @@
         @pl.when(owner)
         def _():
             def one(i, _):
-                j = lax.rem(i + 2 * vel + c + 1, 2 * PLANE)
-                tv, tc = j // 2, j % 2
-                send(own.at[k], dst.at[step_of(vel, tc)], gsend.at[k], grecv.at[k], tv, 2 * y + tc)
+                tz = around(i)
+                for o in (2, 1, 3, 0):
+                    tv = lax.rem(xi + o, ZX) * ZS + tz
+                    for tc in range(2):
+                        at_row = vel if tc == 0 else T - 1 - vel
+                        send(own.at[k], dst.at[at_row], gsend.at[k], grecv.at[k], tv, 2 * y + tc, o == 0)
                 return 0
 
-            lax.fori_loop(0, 2 * PLANE, one, 0)
+            lax.fori_loop(0, ZS, one, 0)
 
     spread(0, mb.at[0])
 
@@ -241,35 +282,45 @@
 
     lax.fori_loop(0, T, cells, jnp.ones((8, 128), F32))
 
+    def left(t, cur):
+        kr[T - 1 - t] = cur
+        return cur * ks[T - 1 - t]
+
+    lax.fori_loop(0, T, left, jnp.ones((8, 128), F32))
+    for s in range(SWEEPS):
+        esrc[s, H:HP] = jnp.zeros((HP - H, 128), F32)
+
     for s in range(SWEEPS):
         remote(mb.at[s], mb.at[s], gsend.at[s], grecv.at[s], vel, gx).wait_recv()
         hi, lo = split(mb[s].reshape(T * NM, 128))
         l3 = jnp.concatenate([hi, lo, hi], axis=1)
         for n in range(NC // 2):
             g = dot(l3, b3[:, 256 * n : 256 * n + 256]).reshape(T, NM, 256)
-            hi, lo = split(jnp.concatenate([g[:, :, 0:128], g[:, :, 128:256]], axis=1))
-            gs[:, 16 * n : 16 * n + 16, :] = hi
-            gs[:, 96 + 16 * n : 112 + 16 * n, :] = hi
-            gs[:, 192 + 16 * n : 208 + 16 * n, :] = lo
+            gs[:, 16 * n : 16 * n + 16, :] = jnp.concatenate([g[:, :, 0:128], g[:, :, 128:256]], axis=1)
+            for d in range(2):
+                hi, lo = split((g[:, :, 128 * d : 128 * d + 128] * kr[...]).reshape(T * NM, 128))
+                r = dot(ec[2 * n + d], jnp.concatenate([hi, lo], axis=1))
+                r = r[0:24, 0:128] + r[24:48, 0:128] + r[0:24, 128:256]
+                esrc[s, pl.ds(2 * n + d, H // NC, stride=NC), :] = r[0 : H // NC]
+
+        for q in (3, 2, 1):
+
+            @pl.when(q > p)
+            def _():
+                ty = jnp.where(c == 0, q, CHIPS - 1 - q)
+                remote(esrc.at[s], ebuf.at[s, p], esend.at[s, q - 1], erecv.at[s, p], vel, 2 * ty + c).start()
 
         def march(u, h):
             t = 2 * u
-            r = dot(a3[:, 0:288], jnp.concatenate([gs[t], gs[t + 1]], axis=1))
+            hi, lo = split(jnp.concatenate([gs[t], gs[t + 1]], axis=1))
+            r = dot(a3[:, 0:288], jnp.concatenate([hi, hi, lo], axis=0))
             a = abc[...].reshape(HP // 8, 8, 128)
             for d in range(2):
                 h = h * (a * ks[t + d][None]) + r[:, 128 * d : 128 * d + 128].reshape(HP // 8, 8, 128)
                 hloc[t + d] = h.reshape(HP, 128)
             return h
 
-        h = lax.fori_loop(0, T // 2, march, jnp.zeros((HP // 8, 8, 128), F32), unroll=2)
-        esrc[s] = h.reshape(HP, 128)
-
-        for q in (3, 2, 1):
-
-            @pl.when(q > p)
-            def _():
-                ty = jnp.where(c == 0, q, CHIPS - 1 - q)
-                remote(esrc.at[s], ebuf.at[s, p], esend.at[s, q - 1], erecv.at[s, p], vel, 2 * ty + c).start()
+        lax.fori_loop(0, T // 2, march, jnp.zeros((HP // 8, 8, 128), F32), unroll=2)
 
         def local_moments(u, _):
             t = 2 * u
@@ -300,14 +351,16 @@
         part[s] = mloc[...] + kc[...] * r.reshape(T, NM, 128)
 
         def rs(i, _):
-            row = lax.rem(i + vel, T)
-            send(
-                part.at[s, step_of(row, c)], rb2.at[s, 2 * vel + c], rsend.at[s + 1], rrecv.at[s + 1],
-                row, 2 * y + row % 2,
-            )
+            tz = around(i)
+            for o in (2, 1, 3, 0):
+                row = lax.rem(xi + o, ZX) * ZS + tz
+                send(
+                    part.at[s, step_of(row, c)], rb2.at[s, 2 * vel + c], rsend.at[s + 1], rrecv.at[s + 1],
+                    row, 2 * y + tz % 2, o == 0,
+                )
             return 0
 
-        lax.fori_loop(0, T, rs, 0)
+        lax.fori_loop(0, ZS, rs, 0)
 
         if s == SWEEPS - 1:
             def finish(t, h):
@@ -345,11 +398,13 @@
     @pl.when(owner)
     def _():
         def one(i, _):
-            tv = lax.rem(i + vel + 1, PLANE)
-            send(own.at[last], mo.at[vel % XS], gsend.at[last], grecv.at[last], tv, 2 * y + section)
+            tz = around(i)
+            for o in (2, 1, 3, 0):
+                tv = lax.rem(xi + o, ZX) * ZS + tz
+                send(own.at[last], mo.at[vel % XS], gsend.at[last], grecv.at[last], tv, 2 * y + section, o == 0)
             return 0
 
-        lax.fori_loop(0, PLANE, one, 0)
+        lax.fori_loop(0, ZS, one, 0)
 
     remote(mo, mo, gsend.at[last], grecv.at[last], vel, gx).wait_recv()
     for x in range(XS):
@@ -393,6 +448,7 @@
     dma = pltpu.SemaphoreType.DMA
     vm = pltpu.VMEM
     scratch = [
+        vm((3, V), F32), vm((1, V), F32),
         vm((XS, V, 128), F32), vm((8, 512), F32), vm((16, 512), BF16), vm((16, 256), BF16),
         vm((NC, 128, 128), F32), vm((HP, 128), F32), vm((2 * CHIPS, XS, 128), jnp.int32),
         vm((XS, NM, 128), F32), vm((SWEEPS, T, NM, 128), F32), vm((SWEEPS + 1, NM, 128), F32),
@@ -400,13 +456,14 @@
         vm((XS, NM, 128), F32),
         vm((384, NC * 128), BF16), vm((HP, 384), BF16), vm((384, 256), F32), vm((HP, 128), F32),
         vm((HP, 128), F32), vm((T, 8, 128), F32), vm((T, 8, 128), F32), vm((CHIPS, 8, 128), F32),
-        vm((T, 8, 256), F32), vm((2 * T * NM, 256), BF16), vm((T, 288, 128), BF16), vm((T, HP, 128), F32),
+        vm((T, 8, 256), F32), vm((2 * T * NM, 256), BF16), vm((T, 96, 128), F32), vm((T, HP, 128), F32),
         vm((T, NM, 128), F32), vm((SWEEPS, CHIPS - 1, HP, 128), F32), vm((SWEEPS, HP, 128), F32),
-        vm((HP, 128), F32),
-        dma((XS,)), dma((2,)), dma, dma, dma((SWEEPS + 1,)), dma((SWEEPS + 1,)), dma((SWEEPS + 1,)),
+        vm((HP, 128), F32), vm((2, 288, 128), F32), vm((NC, 48, 256), BF16), vm((T, 8, 128), F32),
+        dma((XS,)), dma((4,)), dma, dma, dma((SWEEPS + 1,)), dma((SWEEPS + 1,)), dma((SWEEPS + 1,)),
         dma((SWEEPS + 1,)), dma((SWEEPS, CHIPS - 1)), dma((SWEEPS, CHIPS - 1)), dma, dma, dma,
     ]
-    hbm = pl.BlockSpec(memory_space=pl.ANY)
+    hbm = pl.BlockSpec(memory_space=pltpu.MemorySpace.HBM)
+    anywhere = pl.BlockSpec(memory_space=pl.ANY)
     vmem = pl.BlockSpec(memory_space=pltpu.VMEM)
     return pl.pallas_call(
         body,
@@ -414,14 +471,19 @@
             jax.ShapeDtypeStruct((V, XS, 128), F32),
             jax.ShapeDtypeStruct((NM, XS, 128), F32),
         ),
-        in_specs=[hbm, vmem, vmem, pl.BlockSpec(memory_space=pltpu.SMEM), hbm, hbm, hbm],
-        out_specs=(hbm, vmem),
+        in_specs=[hbm] * 3 + [pl.BlockSpec(memory_space=pltpu.SMEM)] + [hbm] * 3,
+        out_specs=(anywhere, vmem),
         scratch_shapes=scratch,
         name="solve",
         compiler_params=pltpu.CompilerParams(
             collective_id=0, has_side_effects=True, vmem_limit_bytes=48 * 2**20
         ),
-    )(distribution, speeds, weights.reshape(1, V), octant, inverses, inflow, solid_cells)
+    )(
+        *(
+            a if a is octant else pltpu.with_memory_space_constraint(a, pltpu.MemorySpace.HBM)
+            for a in (distribution, speeds, weights.reshape(1, V), octant, inverses, inflow, solid_cells)
+        )
+    )
 
 
 def solution(mesh):

time: 76.3 us -> 67.1 us (0.88)
  Pallas kernels: 68.2 us -> 63.3 us
  local copies, waits for them, and re-layouts: 6.56 us -> 2.42 us
    pallas_call x1, Pallas kernels: 68.2 us -> 63.3 us  [per_device(): pl.pallas_call(body, out_shape=(jax.ShapeDtypeStruct((V, XS, 128), F32),...]
    unnamed x12 -> x2, local copies, waits for them, and re-layouts: 6.56 us -> 2.42 us
where the time goes in v2:
time: 67.1 us; the launch traced here: 67 us
  Pallas kernels  63.3 us (94%)
  local copies, waits for them, and re-layouts  2.42 us (4%)
  between operations  1.29 us (2%)
    pallas_call x1, Pallas kernels, per_device(): pl.pallas_call(body, out_shape=(jax.ShapeDtypeStruct((V, XS, 128), F32),...  63.3 us
    unnamed x2, local copies, waits for them, and re-layouts  2.42 us

profile of v2, /device:TPU:1, one launch (start us, length us, event | category | flops | bytes accessed | tf_op | source)
XLA Modules:
  0.0 67.0 jit_solution(15080741954333573075)
XLA Ops:
  1.3 63.3 %solve.1 = (f32[432,16,128]{2,1,0:T(8,128)S(1)}, f32[8,16,128]{2,1,0:T(8,128)S(1)}) custom-call(f32[432,16,128]{2,1,0:T(8,128)} %dist.1, f32[3,432]{1,0:T(4,128)} %speeds_in.1, f32[1,432]{1,0:T(1,128)} %bitcast.1, s32[1]{0:T(128)S(6)} %copy.11.octant, f32[12,128,128]{2,1,0:T(8,128)} %inverses.1, f32[432,128]{1,0:T(8,128)} %inflow.1, s32[16,128]{1,0:T(8,128)} %solid.1), custom_call_target="tpu_custom_call" | custom-call | tf_op jit(solution)/shard_map/solve/pallas_call | solution.py:468
  64.5 1.8 %copy.12 = f32[432,16,128]{2,1,0:T(8,128)} copy(f32[432,16,128]{2,1,0:T(8,128)S(1)} %get-tuple-element.4) | data formatting | bytes 7077888
  66.3 0.6 copy.13

commit v3 on v2

--- a/solution.py
+++ b/solution.py
@@ -27,6 +27,7 @@
 ZX = 4
 ZS = 8
 CHIPS = 4
+PARTS = 3
 
 
 def split(x):
@@ -52,7 +53,7 @@
     dist, speeds_in, weights_in, octant, inverses, inflow, solid,
     out_h, out_m,
     speeds, weights, dx, spd, wall, wdir, inv, infl, sbuf, part0, part, own, rb1, rb2, mb, mo,
-    b3, a3, at, abc, a32, ks, kc, kp, tsc, t2, gs, hloc, mloc, ebuf, esrc, hin, et, ec, kr,
+    b3, a3, at, abc, a32, ks, kc, kp, tsc, t2, gs, hloc, mloc, ebuf, esrc, hin, et, ec, kr, l3, wk, enat, abg,
     dsem, isem, ssend, srecv, rsend, rrecv, gsend, grecv, esend, erecv, osend, orecv, olocal,
 ):
     vel = lax.axis_index("vel")
@@ -66,6 +67,9 @@
 
     def step_of(row, core):
         return jnp.where(core == 0, row, T - 1 - row)
+
+    def classes_of(g):
+        return [(8 * g + i) % NC for i in range(8)]
 
     def remote(src, dst, ss, rs, tv, tg):
         return pltpu.make_async_remote_copy(
@@ -183,18 +187,25 @@
     cls = lax.rem(lax.broadcasted_iota(jnp.int32, (8, 256), 1), NC)
     hi, lo = split(ps)
     hi, lo = hi.astype(F32), lo.astype(F32)
-    for k in range(NC):
-        at[8 * k : 8 * k + 8] = jnp.where(cls == k, hi, 0.0)
-        at[96 + 8 * k : 104 + 8 * k] = jnp.where(cls == k, lo, 0.0)
-        at[192 + 8 * k : 200 + 8 * k] = jnp.where(cls == k, hi, 0.0)
-    at[288:384] = jnp.zeros((96, 256), F32)
-    a3[...] = at[...].T[0:HP].astype(BF16)
     abc[...] = jnp.broadcast_to(rate, (128, 256)).T[0:HP]
+    for g in range(3):
+        for i, k in enumerate(classes_of(g)):
+            at[8 * i : 8 * i + 8] = jnp.where(cls == k, hi, 0.0)
+            at[64 + 8 * i : 72 + 8 * i] = jnp.where(cls == k, lo, 0.0)
+            at[128 + 8 * i : 136 + 8 * i] = jnp.where(cls == k, hi, 0.0)
+        at[192:256] = jnp.zeros((64, 256), F32)
+        table = at[...].T
+        table = [table[8 * (3 * i + g) : 8 * (3 * i + g) + 8] for i in range(9)]
+        table = jnp.concatenate(table + [jnp.zeros((8, 256), F32)], axis=0)
+        a3[g] = table.astype(BF16)
+        for i in range(9):
+            abg[g, i] = abc[8 * (3 * i + g) : 8 * (3 * i + g) + 8]
     pw = abc[...]
     for _ in range(5):
         pw = pw * pw
     a32[...] = pw
     infl[H:HP] = jnp.zeros((HP - H, 128), F32)
+    hloc[:, H:HP, :] = jnp.zeros((T, HP - H, 128), F32)
     infl_copy.wait()
 
     def powers(t, cur):
@@ -287,40 +298,52 @@
         return cur * ks[T - 1 - t]
 
     lax.fori_loop(0, T, left, jnp.ones((8, 128), F32))
-    for s in range(SWEEPS):
-        esrc[s, H:HP] = jnp.zeros((HP - H, 128), F32)
 
     for s in range(SWEEPS):
         remote(mb.at[s], mb.at[s], gsend.at[s], grecv.at[s], vel, gx).wait_recv()
         hi, lo = split(mb[s].reshape(T * NM, 128))
-        l3 = jnp.concatenate([hi, lo, hi], axis=1)
-        for n in range(NC // 2):
-            g = dot(l3, b3[:, 256 * n : 256 * n + 256]).reshape(T, NM, 256)
-            gs[:, 16 * n : 16 * n + 16, :] = jnp.concatenate([g[:, :, 0:128], g[:, :, 128:256]], axis=1)
-            for d in range(2):
-                hi, lo = split((g[:, :, 128 * d : 128 * d + 128] * kr[...]).reshape(T * NM, 128))
-                r = dot(ec[2 * n + d], jnp.concatenate([hi, lo], axis=1))
+        l3[...] = jnp.concatenate([hi, lo, hi], axis=1)
+        for part_of in range(PARTS):
+            for n in range(2 * part_of, 2 * part_of + 2):
+                g = dot(l3[...], b3[:, 256 * n : 256 * n + 256]).reshape(T, NM, 256)
+                gs[:, 16 * n : 16 * n + 16, :] = jnp.concatenate([g[:, :, 0:128], g[:, :, 128:256]], axis=1)
+                for d in range(2):
+                    hi, lo = split((g[:, :, 128 * d : 128 * d + 128] * kr[...]).reshape(T * NM, 128))
+                    wk[2 * n + d] = jnp.concatenate([hi, lo], axis=1)
+            for d in range(4):
+                r = dot(ec[4 * part_of + d], wk[4 * part_of + d])
                 r = r[0:24, 0:128] + r[24:48, 0:128] + r[0:24, 128:256]
-                esrc[s, pl.ds(2 * n + d, H // NC, stride=NC), :] = r[0 : H // NC]
-
-        for q in (3, 2, 1):
-
-            @pl.when(q > p)
-            def _():
-                ty = jnp.where(c == 0, q, CHIPS - 1 - q)
-                remote(esrc.at[s], ebuf.at[s, p], esend.at[s, q - 1], erecv.at[s, p], vel, 2 * ty + c).start()
+                esrc[s, part_of, pl.ds(d, H // NC, stride=4), :] = r[0 : H // NC]
+
+            for gap in (2, 1, 3):
+                q = p + gap
+
+                @pl.when(q < CHIPS)
+                def _():
+                    ty = jnp.where(c == 0, q, CHIPS - 1 - q)
+                    remote(
+                        esrc.at[s, part_of], ebuf.at[s, p, part_of], esend.at[s, gap - 1], erecv.at[s, p],
+                        vel, 2 * ty + c,
+                    ).start()
 
         def march(u, h):
             t = 2 * u
             hi, lo = split(jnp.concatenate([gs[t], gs[t + 1]], axis=1))
-            r = dot(a3[:, 0:288], jnp.concatenate([hi, hi, lo], axis=0))
-            a = abc[...].reshape(HP // 8, 8, 128)
-            for d in range(2):
-                h = h * (a * ks[t + d][None]) + r[:, 128 * d : 128 * d + 128].reshape(HP // 8, 8, 128)
-                hloc[t + d] = h.reshape(HP, 128)
-            return h
-
-        lax.fori_loop(0, T // 2, march, jnp.zeros((HP // 8, 8, 128), F32), unroll=2)
+            after = []
+            for g in range(3):
+                pairs = [k // 2 for k in classes_of(g)[::2]]
+                hs = [hi[16 * n : 16 * n + 16] for n in pairs]
+                ls = [lo[16 * n : 16 * n + 16] for n in pairs]
+                r = dot(a3[g, :, 0:192], jnp.concatenate(hs + hs + ls, axis=0))
+                now = h[g]
+                for d in range(2):
+                    now = now * (abg[g] * ks[t + d][None]) + r[0:72, 128 * d : 128 * d + 128].reshape(9, 8, 128)
+                    for i in range(9):
+                        hloc[t + d, 8 * (3 * i + g) : 8 * (3 * i + g) + 8, :] = now[i]
+                after.append(now)
+            return tuple(after)
+
+        lax.fori_loop(0, T // 2, march, (jnp.zeros((9, 8, 128), F32),) * 3, unroll=2)
 
         def local_moments(u, _):
             t = 2 * u
@@ -338,11 +361,16 @@
 
             @pl.when(q < p)
             def _():
-                remote(esrc.at[s], ebuf.at[s, q], esend.at[s, 0], erecv.at[s, q], vel, gx).wait_recv()
+                full = ebuf.at[s, q]
+                remote(full, full, esend.at[s, 0], erecv.at[s, q], vel, gx).wait_recv()
                 k = kp[jnp.where(c == 0, q, CHIPS - 1 - q)]
                 span = a32[...].reshape(HP // 8, 8, 128) * k[None]
-                now = hin[...].reshape(HP // 8, 8, 128) * span + ebuf[s, q].reshape(HP // 8, 8, 128)
-                hin[...] = now.reshape(HP, 128)
+                now = hin[...].reshape(HP // 8, 8, 128) * span
+                for k in range(NC):
+                    own_rows = pl.ds(k, H // NC, stride=NC)
+                    enat[own_rows, :] = ebuf[s, q, k // 4, pl.ds(k % 4, H // NC, stride=4), :]
+                now = now[0 : H // 8] + enat[...].reshape(H // 8, 8, 128)
+                hin[0:H] = now.reshape(H, 128)
 
         hi, lo = split(hin[...])
         r = dot(t2[:, 0:HP], jnp.concatenate([hi, lo], axis=1))
@@ -426,11 +454,11 @@
     drain(part0, XS, mine, rsend.at[0])
     for s in range(SWEEPS):
         drain(part.at[s], T, owner, rsend.at[s + 1])
-        for q in (3, 2, 1):
-
-            @pl.when(q > p)
+        for gap in (2, 1, 3):
+
+            @pl.when(p + gap < CHIPS)
             def _():
-                remote(esrc.at[s], esrc.at[s], esend.at[s, q - 1], esend.at[s, q - 1], vel, gx).wait_send()
+                remote(esrc.at[s], esrc.at[s], esend.at[s, gap - 1], esend.at[s, gap - 1], vel, gx).wait_send()
 
     @pl.when(owner)
     def _():
@@ -454,18 +482,20 @@
         vm((XS, NM, 128), F32), vm((SWEEPS, T, NM, 128), F32), vm((SWEEPS + 1, NM, 128), F32),
         vm((PLANE, NM, 128), F32), vm((SWEEPS, 2 * PLANE, NM, 128), F32), vm((SWEEPS, T, NM, 128), F32),
         vm((XS, NM, 128), F32),
-        vm((384, NC * 128), BF16), vm((HP, 384), BF16), vm((384, 256), F32), vm((HP, 128), F32),
+        vm((384, NC * 128), BF16), vm((3, 80, 256), BF16), vm((256, 256), F32), vm((HP, 128), F32),
         vm((HP, 128), F32), vm((T, 8, 128), F32), vm((T, 8, 128), F32), vm((CHIPS, 8, 128), F32),
         vm((T, 8, 256), F32), vm((2 * T * NM, 256), BF16), vm((T, 96, 128), F32), vm((T, HP, 128), F32),
-        vm((T, NM, 128), F32), vm((SWEEPS, CHIPS - 1, HP, 128), F32), vm((SWEEPS, HP, 128), F32),
+        vm((T, NM, 128), F32), vm((SWEEPS, CHIPS - 1, PARTS, H // PARTS, 128), F32),
+        vm((SWEEPS, PARTS, H // PARTS, 128), F32),
         vm((HP, 128), F32), vm((2, 288, 128), F32), vm((NC, 48, 256), BF16), vm((T, 8, 128), F32),
+        vm((T * NM, 384), BF16), vm((NC, T * NM, 256), BF16), vm((H, 128), F32), vm((3, 9, 8, 128), F32),
         dma((XS,)), dma((4,)), dma, dma, dma((SWEEPS + 1,)), dma((SWEEPS + 1,)), dma((SWEEPS + 1,)),
         dma((SWEEPS + 1,)), dma((SWEEPS, CHIPS - 1)), dma((SWEEPS, CHIPS - 1)), dma, dma, dma,
     ]
     hbm = pl.BlockSpec(memory_space=pltpu.MemorySpace.HBM)
     anywhere = pl.BlockSpec(memory_space=pl.ANY)
     vmem = pl.BlockSpec(memory_space=pltpu.VMEM)
-    return pl.pallas_call(
+    field, fields = pl.pallas_call(
         body,
         out_shape=(
             jax.ShapeDtypeStruct((V, XS, 128), F32),
@@ -484,6 +514,30 @@
             for a in (distribution, speeds, weights.reshape(1, V), octant, inverses, inflow, solid_cells)
         )
     )
+    parts = 4
+
+    def store(a, b, out_a, out_b, sems):
+        copies = [pltpu.make_async_copy(b, out_b, sems.at[parts])]
+        for i in range(parts):
+            some = pl.ds(i * (V // parts), V // parts)
+            copies.append(pltpu.make_async_copy(a.at[some], out_a.at[some], sems.at[i]))
+        for copy in copies:
+            copy.start()
+        for copy in copies:
+            copy.wait()
+
+    return pl.pallas_call(
+        store,
+        out_shape=(
+            jax.ShapeDtypeStruct(field.shape, F32),
+            jax.ShapeDtypeStruct(fields.shape, F32),
+        ),
+        in_specs=[anywhere, anywhere],
+        out_specs=(hbm, hbm),
+        scratch_shapes=[dma((parts + 1,))],
+        name="store",
+        compiler_params=pltpu.CompilerParams(vmem_limit_bytes=2**20),
+    )(field, fields)
 
 
 def solution(mesh):

time: 67.1 us -> 63.8 us (0.951)
  local copies, waits for them, and re-layouts: 2.42 us -> 0 us
  Pallas kernels: 63.3 us -> 62.4 us
    pallas_call x1, Pallas kernels: 63.3 us -> 60.6 us  [per_device(): pl.pallas_call(body, out_shape=(jax.ShapeDtypeStruct((V, XS, 128), F32),...]
    unnamed x2 -> x0, local copies, waits for them, and re-layouts: 2.42 us -> none
    pallas_call x0 -> x1, Pallas kernels: none -> 1.85 us  [per_device(): pl.pallas_call(store, out_shape=(jax.ShapeDtypeStruct(field.shape, F32),...]
where the time goes in v3:
time: 63.8 us; the launch traced here: 63.7 us
  Pallas kernels  62.4 us (98%)
  between operations  1.28 us (2%)
    pallas_call x1, Pallas kernels, per_device(): pl.pallas_call(body, out_shape=(jax.ShapeDtypeStruct((V, XS, 128), F32),...  60.6 us
    pallas_call x1, Pallas kernels, per_device(): pl.pallas_call(store, out_shape=(jax.ShapeDtypeStruct(field.shape, F32),...  1.85 us

profile of v3, /device:TPU:1, one launch (start us, length us, event | category | flops | bytes accessed | tf_op | source)
XLA Modules:
  0.0 63.7 jit_solution(11660948253589246385)
XLA Ops:
  1.3 60.6 %solve.1 = (f32[432,16,128]{2,1,0:T(8,128)S(1)}, f32[8,16,128]{2,1,0:T(8,128)S(1)}) custom-call(f32[432,16,128]{2,1,0:T(8,128)} %dist.1, f32[3,432]{1,0:T(4,128)} %speeds_in.1, f32[1,432]{1,0:T(1,128)} %bitcast.1, s32[1]{0:T(128)S(6)} %copy.9.octant, f32[12,128,128]{2,1,0:T(8,128)} %inverses.1, f32[432,128]{1,0:T(8,128)} %inflow.1, s32[16,128]{1,0:T(8,128)} %solid.1), custom_call_target="tpu_custom_call" | custom-call | tf_op jit(solution)/shard_map/solve/pallas_call | solution.py:498
  61.9 1.9 %store.1 = (f32[432,16,128]{2,1,0:T(8,128)}, f32[8,16,128]{2,1,0:T(8,128)}) custom-call(f32[432,16,128]{2,1,0:T(8,128)S(1)} %get-tuple-element.4.a, f32[8,16,128]{2,1,0:T(8,128)S(1)} %get-tuple-element.5.b), custom_call_target="tpu_custom_call" | custom-call | tf_op jit(solution)/shard_map/store/pallas_call | solution.py:529

commit v4 on v3

--- a/solution.py
+++ b/solution.py
@@ -52,7 +52,7 @@
 def body(
     dist, speeds_in, weights_in, octant, inverses, inflow, solid,
     out_h, out_m,
-    speeds, weights, dx, spd, wall, wdir, inv, infl, sbuf, part0, part, own, rb1, rb2, mb, mo,
+    speeds, weights, dx, spd, wall, wdir, inv, infl, sbuf, part0, part, own, rb1, first, rb2, mb, mo,
     b3, a3, at, abc, a32, ks, kc, kp, tsc, t2, gs, hloc, mloc, ebuf, esrc, hin, et, ec, kr, l3, wk, enat, abg,
     dsem, isem, ssend, srecv, rsend, rrecv, gsend, grecv, esend, erecv, osend, orecv, olocal,
 ):
@@ -160,8 +160,10 @@
     def rs1(i, _):
         tz = around(i)
         for o in range(2):
-            row = (2 * c + o) * ZS + tz
-            send(part0.at[o * ZS + tz], rb1.at[vel], rsend.at[0], rrecv.at[0], row, 2 * y + tz % 2)
+            tv = (2 * c + o) * ZS + tz
+            for far in range(2):
+                row = o * ZS + lax.rem(tz + far * (ZS // 2), ZS)
+                send(part0.at[row], rb1.at[far, vel], rsend.at[0], rrecv.at[0], tv, 2 * y + tz % 2)
         return 0
 
     lax.fori_loop(0, ZS, rs1, 0)
@@ -236,9 +238,26 @@
         def _():
             full = rb.at[pl.ds(0, n)]
             remote(full, full, rsend.at[k], rrecv.at[k], vel, gx).wait_recv()
-            own[k] = jnp.sum(rb[...].reshape(n // 8, 8, NM, 128), axis=0).sum(axis=0)
-
-    gather(rb1, PLANE, 0, None)
+            own[k - 1] = jnp.sum(rb[...].reshape(n // 8, 8, NM, 128), axis=0).sum(axis=0)
+
+    @pl.when(owner)
+    def _():
+        remote(rb1, rb1, rsend.at[0], rrecv.at[0], vel, gx).wait_recv()
+        for far in range(2):
+            first[far] = jnp.sum(rb1[far].reshape(PLANE // 8, 8, NM, 128), axis=0).sum(axis=0)
+
+        def one(i, _):
+            tz = lax.rem(zi + ZS + (1 - i % 2) * (i // 2 - 2) + (i % 2) * (1 - i // 2), ZS)
+            for o in (2, 1, 3, 0):
+                tv = lax.rem(xi + o, ZX) * ZS + tz
+                for tc in range(2):
+                    for far in range(2):
+                        row = xi * ZS + lax.rem(zi + far * (ZS // 2), ZS)
+                        at_row = row if tc == 0 else T - 1 - row
+                        send(first.at[far], mb.at[0, at_row], gsend.at[0], grecv.at[0], tv, 2 * y + tc, o == 0)
+            return 0
+
+        lax.fori_loop(0, 4, one, 0)
 
     def spread(k, dst):
         @pl.when(owner)
@@ -249,12 +268,11 @@
                     tv = lax.rem(xi + o, ZX) * ZS + tz
                     for tc in range(2):
                         at_row = vel if tc == 0 else T - 1 - vel
-                        send(own.at[k], dst.at[at_row], gsend.at[k], grecv.at[k], tv, 2 * y + tc, o == 0)
+                        send(own.at[k - 1], dst.at[at_row], gsend.at[k], grecv.at[k], tv, 2 * y + tc, o == 0)
                 return 0
 
             lax.fori_loop(0, ZS, one, 0)
 
-    spread(0, mb.at[0])
 
     inv_copy.wait()
     ii = lax.broadcasted_iota(jnp.int32, (128, 128), 0)
@@ -343,7 +361,7 @@
                 after.append(now)
             return tuple(after)
 
-        lax.fori_loop(0, T // 2, march, (jnp.zeros((9, 8, 128), F32),) * 3, unroll=2)
+        lax.fori_loop(0, T // 2, march, (jnp.zeros((9, 8, 128), F32),) * 3, unroll=4)
 
         def local_moments(u, _):
             t = 2 * u
@@ -354,7 +372,7 @@
             mloc[t + 1] = r[:, 128:256]
             return 0
 
-        lax.fori_loop(0, T // 2, local_moments, 0, unroll=2)
+        lax.fori_loop(0, T // 2, local_moments, 0, unroll=4)
 
         hin[...] = infl[...]
         for q in range(CHIPS - 1):
@@ -397,20 +415,20 @@
                 hloc[t] = (hloc[t].reshape(HP // 8, 8, 128) + h).reshape(HP, 128)
                 return h
 
-            first = pl.multiple_of(c * H, 8)
+            start = pl.multiple_of(c * H, 8)
 
             def far(t, h):
                 h = finish(t, h)
                 x = jnp.where(c == 0, t - XS, T - 1 - t)
                 remote(
-                    hloc.at[t, pl.ds(0, H)], out_h.at[pl.ds(first, H), x, :], osend, orecv, vel, 2 * y + 1 - c
+                    hloc.at[t, pl.ds(0, H)], out_h.at[pl.ds(start, H), x, :], osend, orecv, vel, 2 * y + 1 - c
                 ).start()
                 return h
 
             def near(t, h):
                 h = finish(t, h)
                 x = jnp.where(c == 0, t, XS - 1 - t)
-                pltpu.make_async_copy(hloc.at[t, pl.ds(0, H)], out_h.at[pl.ds(first, H), x, :], olocal).start()
+                pltpu.make_async_copy(hloc.at[t, pl.ds(0, H)], out_h.at[pl.ds(start, H), x, :], olocal).start()
                 return h
 
             h = lax.fori_loop(0, XS, near, hin[...].reshape(HP // 8, 8, 128))
@@ -429,7 +447,7 @@
             tz = around(i)
             for o in (2, 1, 3, 0):
                 tv = lax.rem(xi + o, ZX) * ZS + tz
-                send(own.at[last], mo.at[vel % XS], gsend.at[last], grecv.at[last], tv, 2 * y + section, o == 0)
+                send(own.at[last - 1], mo.at[vel % XS], gsend.at[last], grecv.at[last], tv, 2 * y + section, o == 0)
             return 0
 
         lax.fori_loop(0, ZS, one, 0)
@@ -442,16 +460,16 @@
         remote(solid, sbuf.at[gx], ssend, srecv, vel, gx).wait_send()
     mine = owner & (section == c)
 
-    def drain(buf, n, less, sem):
+    def drain(buf, n, less, sem, by=1):
         @pl.when(less)
         def _():
-            remote(buf.at[pl.ds(0, n - 1)], buf.at[pl.ds(0, n - 1)], sem, sem, vel, gx).wait_send()
+            remote(buf.at[pl.ds(0, n - by)], buf.at[pl.ds(0, n - by)], sem, sem, vel, gx).wait_send()
 
         @pl.when(jnp.logical_not(less))
         def _():
             remote(buf.at[pl.ds(0, n)], buf.at[pl.ds(0, n)], sem, sem, vel, gx).wait_send()
 
-    drain(part0, XS, mine, rsend.at[0])
+    drain(rb1.at[0], 2 * XS, mine, rsend.at[0], 2)
     for s in range(SWEEPS):
         drain(part.at[s], T, owner, rsend.at[s + 1])
         for gap in (2, 1, 3):
@@ -463,7 +481,7 @@
     @pl.when(owner)
     def _():
         for k in range(SWEEPS):
-            few = rb2.at[0, pl.ds(0, 2 * PLANE - 1)]
+            few = rb2.at[0, pl.ds(0, 2 * PLANE - (2 if k == 0 else 1))]
             remote(few, few, gsend.at[k], gsend.at[k], vel, gx).wait_send()
         drain(rb2.at[0], PLANE, section == c, gsend.at[last])
 
@@ -479,8 +497,8 @@
         vm((3, V), F32), vm((1, V), F32),
         vm((XS, V, 128), F32), vm((8, 512), F32), vm((16, 512), BF16), vm((16, 256), BF16),
         vm((NC, 128, 128), F32), vm((HP, 128), F32), vm((2 * CHIPS, XS, 128), jnp.int32),
-        vm((XS, NM, 128), F32), vm((SWEEPS, T, NM, 128), F32), vm((SWEEPS + 1, NM, 128), F32),
-        vm((PLANE, NM, 128), F32), vm((SWEEPS, 2 * PLANE, NM, 128), F32), vm((SWEEPS, T, NM, 128), F32),
+        vm((XS, NM, 128), F32), vm((SWEEPS, T, NM, 128), F32), vm((SWEEPS, NM, 128), F32),
+        vm((2, PLANE, NM, 128), F32), vm((2, NM, 128), F32), vm((SWEEPS, 2 * PLANE, NM, 128), F32), vm((SWEEPS, T, NM, 128), F32),
         vm((XS, NM, 128), F32),
         vm((384, NC * 128), BF16), vm((3, 80, 256), BF16), vm((256, 256), F32), vm((HP, 128), F32),
         vm((HP, 128), F32), vm((T, 8, 128), F32), vm((T, 8, 128), F32), vm((CHIPS, 8, 128), F32),

time: 63.8 us -> 62.8 us (0.984)
  Pallas kernels: 62.4 us -> 61.4 us
    pallas_call x1, Pallas kernels: 60.6 us -> 59.5 us  [per_device(): pl.pallas_call(body, out_shape=(jax.ShapeDtypeStruct((V, XS, 128), F32),...]
where the time goes in v4:
time: 62.8 us; the launch traced here: 62.7 us
  Pallas kernels  61.4 us (98%)
  between operations  1.28 us (2%)
    pallas_call x1, Pallas kernels, per_device(): pl.pallas_call(body, out_shape=(jax.ShapeDtypeStruct((V, XS, 128), F32),...  59.5 us
    pallas_call x1, Pallas kernels, per_device(): pl.pallas_call(store, out_shape=(jax.ShapeDtypeStruct(field.shape, F32),...  1.85 us

profile of v4, /device:TPU:1, one launch (start us, length us, event | category | flops | bytes accessed | tf_op | source)
XLA Modules:
  0.0 62.7 jit_solution(12245184400971706559)
XLA Ops:
  1.3 59.5 %solve.1 = (f32[432,16,128]{2,1,0:T(8,128)S(1)}, f32[8,16,128]{2,1,0:T(8,128)S(1)}) custom-call(f32[432,16,128]{2,1,0:T(8,128)} %dist.1, f32[3,432]{1,0:T(4,128)} %speeds_in.1, f32[1,432]{1,0:T(1,128)} %bitcast.1, s32[1]{0:T(128)S(6)} %copy.9.octant, f32[12,128,128]{2,1,0:T(8,128)} %inverses.1, f32[432,128]{1,0:T(8,128)} %inflow.1, s32[16,128]{1,0:T(8,128)} %solid.1), custom_call_target="tpu_custom_call" | custom-call | tf_op jit(solution)/shard_map/solve/pallas_call | solution.py:516
  60.8 1.9 %store.1 = (f32[432,16,128]{2,1,0:T(8,128)}, f32[8,16,128]{2,1,0:T(8,128)}) custom-call(f32[432,16,128]{2,1,0:T(8,128)S(1)} %get-tuple-element.4.a, f32[8,16,128]{2,1,0:T(8,128)S(1)} %get-tuple-element.5.b), custom_call_target="tpu_custom_call" | custom-call | tf_op jit(solution)/shard_map/store/pallas_call | solution.py:547

commit v5 on v4

--- a/solution.py
+++ b/solution.py
@@ -361,7 +361,7 @@
                 after.append(now)
             return tuple(after)
 
-        lax.fori_loop(0, T // 2, march, (jnp.zeros((9, 8, 128), F32),) * 3, unroll=4)
+        lax.fori_loop(0, T // 2, march, (jnp.zeros((9, 8, 128), F32),) * 3, unroll=8)
 
         def local_moments(u, _):
             t = 2 * u
@@ -372,7 +372,7 @@
             mloc[t + 1] = r[:, 128:256]
             return 0
 
-        lax.fori_loop(0, T // 2, local_moments, 0, unroll=4)
+        lax.fori_loop(0, T // 2, local_moments, 0, unroll=8)
 
         hin[...] = infl[...]
         for q in range(CHIPS - 1):

time: 62.8 us -> 62.5 us (level)
  no operation moved by 1% of the time
where the time goes in v5:
time: 62.5 us; the launch traced here: 62.4 us
  Pallas kernels  61.1 us (98%)
  between operations  1.28 us (2%)
    pallas_call x1, Pallas kernels, per_device(): pl.pallas_call(body, out_shape=(jax.ShapeDtypeStruct((V, XS, 128), F32),...  59.3 us
    pallas_call x1, Pallas kernels, per_device(): pl.pallas_call(store, out_shape=(jax.ShapeDtypeStruct(field.shape, F32),...  1.85 us

profile of v5, /device:TPU:1, one launch (start us, length us, event | category | flops | bytes accessed | tf_op | source)
XLA Modules:
  0.0 62.4 jit_solution(13277878184812974633)
XLA Ops:
  1.3 59.3 %solve.1 = (f32[432,16,128]{2,1,0:T(8,128)S(1)}, f32[8,16,128]{2,1,0:T(8,128)S(1)}) custom-call(f32[432,16,128]{2,1,0:T(8,128)} %dist.1, f32[3,432]{1,0:T(4,128)} %speeds_in.1, f32[1,432]{1,0:T(1,128)} %bitcast.1, s32[1]{0:T(128)S(6)} %copy.9.octant, f32[12,128,128]{2,1,0:T(8,128)} %inverses.1, f32[432,128]{1,0:T(8,128)} %inflow.1, s32[16,128]{1,0:T(8,128)} %solid.1), custom_call_target="tpu_custom_call" | custom-call | tf_op jit(solution)/shard_map/solve/pallas_call | solution.py:516
  60.5 1.9 %store.1 = (f32[432,16,128]{2,1,0:T(8,128)}, f32[8,16,128]{2,1,0:T(8,128)}) custom-call(f32[432,16,128]{2,1,0:T(8,128)S(1)} %get-tuple-element.4.a, f32[8,16,128]{2,1,0:T(8,128)S(1)} %get-tuple-element.5.b), custom_call_target="tpu_custom_call" | custom-call | tf_op jit(solution)/shard_map/store/pallas_call | solution.py:547
